TPU v7x, 32 devices: a whole 2x2x4 slice. The times are simulated.
32 devices in a mesh: col: 4 (over y, x), wide: 8 (over z, core).
Axes of the slice: x: 2, y: 2, z: 4, core: 2. Of those that a mesh axis runs over, the one named last changes fastest.
Arguments:
- flux_jac: bfloat16 [768, 320, 320], P(('col', 'wide')), may hold values from -0.3125 to 0.3125
- dissipation: float32 [768], P(('col', 'wide')), may hold values from 0.1 to 0.4
- basis: bfloat16 [512, 320, 128], P(('col', 'wide')), may hold values from -0.5 to 0.5
- residual: bfloat16 [64, 2560], P(('col', 'wide')), may hold values from -6 to 6
- face_elems: int32 [768, 2], P(('col', 'wide')), may hold values from 0 to 7, as said below
- primal: int32 [64, 128], P(('col', 'wide')), may hold values from 0 to 4095, as said below
- coarse_owner: int32 [4096], replicated, may hold values from 0 to 4095, as said below
- counts: int32 [64], P(('col', 'wide')), may hold values from 32 to 128, as said below
Outputs:
- correction: float32 [64, 2560], P(('col', 'wide'))
- coarse_solution: float32 [4096], P(('col', 'wide'))
Inputs may be any that keep to these rules, and one draw needn't show every extreme that they name: `face_elems`: local element numbers inside the face's subdomain; the two elements of a face differ. `primal`: the 128 entries of a subdomain are distinct. Among the live entries (position below counts) of the subdomains of one device, at most 64 have coarse_owner slots in one owner column (slot // 1024), and in every draw some devices reach 64 for every owner column. `coarse_owner`: A permutation of the 4096 slots. Slot t belongs to owner column t // 1024, and to the device with index t // 128 along col+wide. `counts`: in every draw all subdomains of some wide index have 128 live constraints.
All inputs are finite; a program needn't handle non-finite values.
Results may differ from a plain program's by a relative error of at most 0.0042.
Values may be sent and summed in bfloat16 or wider, within the bound.
A program may use at most 64 MiB of HBM per device.

v0:
```python
import jax
import jax.numpy as jnp
from jax import lax
from jax.sharding import PartitionSpec as P

ITERS = 3


damping = 0.7


def body(flux_jac, dissipation, basis, residual, face_elems, primal, coarse_owner, counts):
    col_count = lax.axis_size("col")
    wide_count = lax.axis_size("wide")
    sub_count = residual.shape[0]
    face_count = flux_jac.shape[0]
    face_sub = face_count // sub_count
    elem_count = basis.shape[0]
    elem_sub = elem_count // sub_count
    unit_count = basis.shape[1]
    prim_count = basis.shape[2]
    slot_count = coarse_owner.shape[0]
    per_col = slot_count // col_count
    per_dev = per_col // wide_count
    capacity = sub_count * prim_count // col_count
    row_count = sub_count * prim_count
    owner_sub = jnp.arange(face_count, dtype=jnp.int32) // face_sub
    elem_a = owner_sub * elem_sub + face_elems[:, 0]
    elem_b = owner_sub * elem_sub + face_elems[:, 1]
    basis_a = jnp.take(basis, elem_a, axis=0)
    basis_b = jnp.take(basis, elem_b, axis=0)
    paired = (basis_a.astype(jnp.float32) + basis_b.astype(jnp.float32)).astype(jnp.bfloat16)
    flux_term = jnp.einsum("fij,fjp->fip", flux_jac, paired, preferred_element_type=jnp.float32)
    jump_term = basis_a.astype(jnp.float32) - basis_b.astype(jnp.float32)
    face_term = 0.5 * flux_term + (0.5 * dissipation)[:, None, None] * jump_term
    elem_onehot = (elem_a[None, :] == jnp.arange(elem_count, dtype=jnp.int32)[:, None]).astype(
        jnp.float32
    )
    elem_image = jnp.einsum(
        "ef,fnp->enp", elem_onehot, face_term, precision=lax.Precision.HIGHEST
    ).astype(jnp.bfloat16)
    basis_sub = basis.reshape(sub_count, elem_sub * unit_count, prim_count)
    image_sub = elem_image.reshape(sub_count, elem_sub * unit_count, prim_count)
    alive_bool = jnp.arange(prim_count, dtype=jnp.int32)[None, :] < counts[:, None]
    alive_mask = alive_bool.astype(jnp.float32)
    schur_block = jnp.einsum(
        "snp,snq->spq", basis_sub, image_sub, preferred_element_type=jnp.float32
    )
    schur_block = schur_block * alive_mask[:, :, None] * alive_mask[:, None, :]
    load_vec = (
        jnp.einsum("snp,sn->sp", basis_sub, residual, preferred_element_type=jnp.float32)
        * alive_mask
    )
    diag_vals = jnp.diagonal(schur_block, axis1=1, axis2=2)
    slot_of = jnp.take(coarse_owner, primal)
    owner_col = slot_of // per_col
    local_row = slot_of % per_col
    alive_flat = alive_bool.reshape(row_count)
    flat_owner = owner_col.reshape(row_count)
    dest_hits = (
        (flat_owner[:, None] == jnp.arange(col_count, dtype=jnp.int32)[None, :])
        & alive_flat[:, None]
    ).astype(jnp.int32)
    before = jnp.cumsum(dest_hits, axis=0) - dest_hits
    position = jnp.sum(before * dest_hits, axis=1)
    target = jnp.where(alive_flat, flat_owner * capacity + position, col_count * capacity)
    from_sub = jnp.arange(row_count, dtype=jnp.int32) // prim_count
    send_vals = (
        jnp.zeros((col_count * capacity, prim_count), jnp.float32)
        .at[target]
        .set(schur_block.reshape(row_count, prim_count), mode="drop")
    )
    send_load = (
        jnp.zeros((col_count * capacity,), jnp.float32)
        .at[target]
        .set(load_vec.reshape(row_count), mode="drop")
    )
    send_diag = (
        jnp.zeros((col_count * capacity,), jnp.float32)
        .at[target]
        .set(diag_vals.reshape(row_count), mode="drop")
    )
    send_row = (
        jnp.zeros((col_count * capacity,), jnp.int32)
        .at[target]
        .set(local_row.reshape(row_count), mode="drop")
    )
    send_from = jnp.zeros((col_count * capacity,), jnp.int32).at[target].set(from_sub, mode="drop")
    send_cols = jnp.broadcast_to(slot_of[None], (col_count, sub_count, prim_count)).reshape(
        col_count * sub_count, prim_count
    )
    recv_vals, recv_load, recv_diag, recv_row, recv_from, recv_cols = (
        lax.all_to_all(send_vals, "col", split_axis=0, concat_axis=0, tiled=True),
        lax.all_to_all(send_load, "col", split_axis=0, concat_axis=0, tiled=True),
        lax.all_to_all(send_diag, "col", split_axis=0, concat_axis=0, tiled=True),
        lax.all_to_all(send_row, "col", split_axis=0, concat_axis=0, tiled=True),
        lax.all_to_all(send_from, "col", split_axis=0, concat_axis=0, tiled=True),
        lax.all_to_all(send_cols, "col", split_axis=0, concat_axis=0, tiled=True),
    )
    block_load = jax.ops.segment_sum(recv_load, recv_row, num_segments=per_col)
    block_diag = jax.ops.segment_sum(recv_diag, recv_row, num_segments=per_col)
    pick_mask = (
        recv_from.reshape(col_count, capacity)[:, :, None]
        == jnp.arange(sub_count, dtype=jnp.int32)[None, None, :]
    )
    col_load, col_diag = lax.psum((block_load, block_diag), "wide")
    diag_floor = jnp.maximum(col_diag, 1.0)
    col_part = damping * col_load / diag_floor
    for sweep_idx in range(ITERS):
        solution_all = lax.all_gather(col_part, "col", axis=0, tiled=True)
        gathered = jnp.take(solution_all, recv_cols).reshape(col_count, sub_count, prim_count)
        paired_rows = jnp.einsum(
            "ncp,nsp->ncs",
            recv_vals.reshape(col_count, capacity, prim_count),
            gathered,
            precision=lax.Precision.HIGHEST,
        )
        row_value = jnp.sum(jnp.where(pick_mask, paired_rows, 0.0), axis=2).reshape(
            col_count * capacity
        )
        col_prod = lax.psum(jax.ops.segment_sum(row_value, recv_row, num_segments=per_col), "wide")
        col_part = col_part + damping * (col_load - col_prod) / diag_floor
    final_all = lax.all_gather(col_part.astype(jnp.bfloat16), "col", axis=0, tiled=True)
    coarse_solution = lax.dynamic_slice_in_dim(col_part, lax.axis_index("wide") * per_dev, per_dev)
    near_sol = jnp.where(alive_bool, jnp.take(final_all, slot_of), jnp.zeros((), jnp.bfloat16))
    correction = jnp.einsum("snp,sp->sn", basis_sub, near_sol, preferred_element_type=jnp.float32)
    return (correction, coarse_solution)


def solution(mesh):
    return jax.shard_map(
        body,
        mesh=mesh,
        in_specs=(
            P(("col", "wide"), None, None),
            P(("col", "wide")),
            P(("col", "wide"), None, None),
            P(("col", "wide"), None),
            P(("col", "wide"), None),
            P(("col", "wide"), None),
            P(),
            P(("col", "wide")),
        ),
        out_specs=(P(("col", "wide"), None), P(("col", "wide"))),
        check_vma=False,
    )
```

profile of v0, /device:TPU:0, one launch (start us, length us, event | category | flops | bytes accessed | tf_op | source)
XLA Modules:
  0.0 196.7 jit_solution(12198145800826417601)
XLA Ops:
  0.6 0.8 fusion.51
  1.4 2.0 gather_fusion
  3.4 0.7 fusion.50
  4.1 0.8 compare_and_fusion.2
  4.9 0.7 bitcast_add_fusion.1
  5.6 0.7 fusion.53
  6.3 1.2 reduce-window.6
  7.6 0.1 copy.22
  8.0 0.9 gather_fusion.3
  8.9 2.1 %gather_fusion.4 = bf16[24,320,128]{2,1,0:T(8,128)(2,1)} fusion(bf16[16,320,128]{2,1,0:T(8,128)(2,1)S(1)} %copy-done, s32[1024]{0:T(1024)S(1)} %get-tuple-element.24), kind=kCustom, calls=%fused_computation.2.clone | custom fusion | bytes 3932256 | tf_op jit(solution)/shard_map/jit(_take)/gather | solution.py:31
  11.1 6.0 %fusion.2 = f32[24,320,128]{2,1,0:T(8,128)S(1)} fusion(bf16[24,320,320]{2,1,0:T(8,128)(2,1)} %param.12, bf16[24,320,128]{2,1,0:T(8,128)(2,1)} %gather_fusion.4, bf16[24,320,128]{2,1,0:T(8,128)(2,1)S(1)} %gather_fusion.3, f32[24]{0:T(128)S(1)} %broadcast_multiply_fusion, pred[24]{0:T(512)(128)(4,1)S(1)} %get-tuple-element.16, ...), kind=kOutput, calls=%fused_computation.22 | convolution fusion | flops 642908160 | bytes 12779664 | tf_op jit(solution)/shard_map/fij,fjp->fip/dot_general | solution.py:33
  17.1 3.9 %fusion.10 = bf16[16,320,128]{2,0,1:T(8,128)(2,1)S(1)} fusion(f32[24,320,128]{2,1,0:T(8,128)S(1)} %fusion.2, s32[24]{0:T(128)S(1)} %bitcast_add_fusion.1), kind=kOutput, calls=%fused_computation.29 | convolution fusion | flops 189399424 | bytes 5242976 | tf_op jit(solution)/shard_map/ef,fnp->enp/dot_general | solution.py:39
  21.0 0.3 copy.27
  21.3 0.6 fusion.13
  21.9 4.6 %copy.29 = f32[2,128,128]{0,2,1:T(8,128)} copy(f32[2,128,128]{2,1,0:T(8,128)S(1)} %bitcast.134) | data formatting | bytes 262144 | tf_op jit(solution)/shard_map/mul | solution.py:49
  26.6 1.8 gather_fusion.1
  28.5 1.4 scatter_custom_fusion.3
  29.9 0.7 all_to_all.45
  30.6 5.2 %all-to-all-start.2 = ((f32[4,64,1]{1,2,0:T(1,128)}), f32[4,64,1]{1,2,0:T(1,128)S(1)}, u32[]{:S(2)}, u32[]{:S(2)}) async-start(f32[4,64,1]{1,2,0:T(1,128)} %bitcast.25), calls=%async_computation.2 | async-start | bytes 4096 | tf_op jit(solution)/shard_map/all_to_all | solution.py:95
  35.7 0.3 fusion.20
  36.1 1.4 scatter_custom_fusion
  37.5 0.7 all_to_all.40
  38.2 2.1 %all-to-all-done.2 = f32[4,64,1]{1,2,0:T(1,128)S(1)} async-done(((f32[4,64,1]{1,2,0:T(1,128)}), f32[4,64,1]{1,2,0:T(1,128)S(1)}, u32[]{:S(2)}, u32[]{:S(2)}) %all-to-all-start.2) | async-done | bytes 1056 | tf_op jit(solution)/shard_map/all_to_all | solution.py:95
  40.2 3.4 %all-to-all-start = ((s32[4,64,1]{1,2,0:T(1,128)}), s32[4,64,1]{1,2,0:T(1,128)S(1)}, u32[]{:S(2)}, u32[]{:S(2)}) async-start(s32[4,64,1]{1,2,0:T(1,128)} %bitcast.9), calls=%async_computation | async-start | bytes 4096 | tf_op jit(solution)/shard_map/all_to_all | solution.py:96
  43.6 1.4 scatter_custom_fusion.1
  45.1 0.7 all_to_all.42
  45.7 1.7 scatter_custom_fusion.6
  47.5 1.4 scatter_custom_fusion.5
  48.9 0.7 all_to_all.48
  49.5 4.1 %all-to-all-start.1 = ((f32[4,64,1]{1,2,0:T(1,128)}), f32[4,64,1]{1,2,0:T(1,128)S(1)}, u32[]{:S(2)}, u32[]{:S(2)}) async-start(f32[4,64,1]{1,2,0:T(1,128)} %bitcast.15), calls=%async_computation.1 | async-start | bytes 4096 | tf_op jit(solution)/shard_map/all_to_all | solution.py:94
  53.7 0.6 broadcast.421
  54.3 0.6 reduce.11
  55.0 0.5 broadcast.420
  55.5 0.7 reduce.9
  56.2 2.1 %all-to-all-done.1 = f32[4,64,1]{1,2,0:T(1,128)S(1)} async-done(((f32[4,64,1]{1,2,0:T(1,128)}), f32[4,64,1]{1,2,0:T(1,128)S(1)}, u32[]{:S(2)}, u32[]{:S(2)}) %all-to-all-start.1) | async-done | bytes 1056 | tf_op jit(solution)/shard_map/all_to_all | solution.py:94
  58.3 0.6 broadcast_in_dim.82
  58.9 3.2 %all-to-all-start.5 = ((s32[4,2,128]{2,1,0:T(2,128)}), s32[4,2,128]{2,1,0:T(2,128)S(1)}, u32[]{:S(2)}, u32[]{:S(2)}) async-start(s32[4,2,128]{2,1,0:T(2,128)} %broadcast_in_dim.82), calls=%async_computation.5 | async-start | bytes 8192 | tf_op jit(solution)/shard_map/all_to_all | solution.py:98
  62.2 0.6 reduce.10
  62.9 2.3 %scatter_custom_fusion.4 = f32[1024]{0:T(1024)S(1)} fusion(s32[256]{0:T(256)S(1)} %reshape.392, f32[256]{0:T(256)S(1)} %reshape.410, f32[]{:T(128)} %constant.118.clone.1), kind=kCustom, calls=%fused_computation.88 | custom fusion | flops 256 | bytes 4100 | tf_op jit(solution)/shard_map/scatter-add | solution.py:101
  65.2 2.3 %scatter_custom_fusion.2 = f32[1024]{0:T(1024)S(1)} fusion(s32[256]{0:T(256)S(1)} %reshape.392, f32[256]{0:T(256)S(1)} %reshape.394, f32[]{:T(128)} %constant.118.clone.1), kind=kCustom, calls=%fused_computation.90 | custom fusion | flops 256 | bytes 4100 | tf_op jit(solution)/shard_map/scatter-add | solution.py:100
  67.6 13.8 %all-reduce = (f32[1024]{0:T(1024)S(1)}, f32[1024]{0:T(1024)S(1)}) all-reduce(f32[1024]{0:T(1024)S(1)} %scatter_custom_fusion.2, f32[1024]{0:T(1024)S(1)} %scatter_custom_fusion.4), channel_id=1, replica_groups=mesh['col'=4,'wide'=8] {'wide'}, use_global_device_ids=true, to_apply=%region_6.7 | all-reduce | flops 2048 | bytes 16384 | tf_op jit(solution)/shard_map/psum | solution.py:106
  81.4 8.6 %all_gather.12 = f32[4096]{0:T(1024)S(1)} all-gather(f32[1024]{0:T(1024)S(1)} %multiply_divide_fusion), channel_id=1, replica_groups=mesh['col'=4,'wide'=8] {'col'}, dimensions={0}, use_global_device_ids=true | all-gather | bytes 20480 | tf_op jit(solution)/shard_map/all_gather | solution.py:110
  90.1 3.2 %all-to-all-start.3 = ((s32[4,64,1]{1,2,0:T(1,128)}), s32[4,64,1]{1,2,0:T(1,128)S(1)}, u32[]{:S(2)}, u32[]{:S(2)}) async-start(s32[4,64,1]{1,2,0:T(1,128)} %all_to_all.48), calls=%async_computation.3 | async-start | bytes 4096 | tf_op jit(solution)/shard_map/all_to_all | solution.py:97
  93.3 6.2 %gather_fusion.5 = f32[1024]{0:T(1024)S(1)} fusion(f32[4096]{0:T(1024)S(1)} %all_gather.12, s32[1024]{0:T(1024)S(1)} %bitcast_clamp_fusion), kind=kCustom, calls=%fused_computation.1.clone | custom fusion | bytes 12288 | tf_op jit(solution)/shard_map/jit(_take)/gather | solution.py:111
  99.5 4.2 %all-to-all-start.4 = ((f32[4,64,128]{2,1,0:T(8,128)}), f32[4,64,128]{2,1,0:T(8,128)S(1)}, u32[]{:S(2)}, u32[]{:S(2)}) async-start(f32[4,64,128]{2,1,0:T(8,128)} %bitcast.28), calls=%async_computation.4 | async-start | bytes 262144 | tf_op jit(solution)/shard_map/all_to_all | solution.py:93
  103.7 5.0 %all-to-all-done.4 = f32[4,64,128]{2,1,0:T(8,128)S(1)} async-done(((f32[4,64,128]{2,1,0:T(8,128)}), f32[4,64,128]{2,1,0:T(8,128)S(1)}, u32[]{:S(2)}, u32[]{:S(2)}) %all-to-all-start.4) | async-done | bytes 131104 | tf_op jit(solution)/shard_map/all_to_all | solution.py:93
  108.7 0.3 fusion.14
  109.1 2.3 %scatter_custom_fusion.7 = f32[1024]{0:T(1024)S(1)} fusion(s32[256]{0:T(256)S(1)} %reshape.392, f32[256]{0:T(256)S(1)} %reshape.434, f32[]{:T(128)} %constant.118.clone.1), kind=kCustom, calls=%fused_computation.86 | custom fusion | flops 256 | bytes 4100 | tf_op jit(solution)/shard_map/scatter-add | solution.py:121
  111.4 13.6 %psum.37 = f32[1024]{0:T(1024)S(1)} all-reduce(f32[1024]{0:T(1024)S(1)} %scatter_custom_fusion.7), channel_id=1, replica_groups=mesh['col'=4,'wide'=8] {'wide'}, use_global_device_ids=true, to_apply=%region_14.17 | all-reduce | flops 1024 | bytes 8192 | tf_op jit(solution)/shard_map/psum | solution.py:121
  125.0 7.6 %all_gather.13 = f32[4096]{0:T(1024)S(1)} all-gather(f32[1024]{0:T(1024)S(1)} %divide_add_fusion.2), channel_id=1, replica_groups=mesh['col'=4,'wide'=8] {'col'}, dimensions={0}, use_global_device_ids=true | all-gather | bytes 20480 | tf_op jit(solution)/shard_map/all_gather | solution.py:110
  132.6 6.1 %gather_fusion.6 = f32[1024]{0:T(1024)S(1)} fusion(f32[4096]{0:T(1024)S(1)} %all_gather.13, s32[1024]{0:T(1024)S(1)} %bitcast_clamp_fusion), kind=kCustom, calls=%fused_computation.3.clone | custom fusion | bytes 12288 | tf_op jit(solution)/shard_map/jit(_take)/gather | solution.py:111
  138.7 0.3 fusion.15
  139.2 2.3 %scatter_custom_fusion.8 = f32[1024]{0:T(1024)S(1)} fusion(s32[256]{0:T(256)S(1)} %reshape.392, f32[256]{0:T(256)S(1)} %reshape.442, f32[]{:T(128)} %constant.118.clone.1), kind=kCustom, calls=%fused_computation.84 | custom fusion | flops 256 | bytes 4100 | tf_op jit(solution)/shard_map/scatter-add | solution.py:121
  141.5 13.6 %psum.38 = f32[1024]{0:T(1024)S(1)} all-reduce(f32[1024]{0:T(1024)S(1)} %scatter_custom_fusion.8), channel_id=1, replica_groups=mesh['col'=4,'wide'=8] {'wide'}, use_global_device_ids=true, to_apply=%region_17.20 | all-reduce | flops 1024 | bytes 8192 | tf_op jit(solution)/shard_map/psum | solution.py:121
  155.1 8.0 %all_gather.14 = f32[4096]{0:T(1024)S(1)} all-gather(f32[1024]{0:T(1024)S(1)} %divide_add_fusion.1), channel_id=1, replica_groups=mesh['col'=4,'wide'=8] {'col'}, dimensions={0}, use_global_device_ids=true | all-gather | bytes 20480 | tf_op jit(solution)/shard_map/all_gather | solution.py:110
  163.1 6.1 %gather_fusion.7 = f32[1024]{0:T(1024)S(1)} fusion(f32[4096]{0:T(1024)S(1)} %all_gather.14, s32[1024]{0:T(1024)S(1)} %bitcast_clamp_fusion), kind=kCustom, calls=%fused_computation.4.clone | custom fusion | bytes 12288 | tf_op jit(solution)/shard_map/jit(_take)/gather | solution.py:111
  169.3 0.3 fusion.16
  169.7 2.3 %scatter_custom_fusion.9 = f32[1024]{0:T(1024)S(1)} fusion(s32[256]{0:T(256)S(1)} %reshape.392, f32[256]{0:T(256)S(1)} %reshape.450, f32[]{:T(128)} %constant.118.clone.1), kind=kCustom, calls=%fused_computation.82 | custom fusion | flops 256 | bytes 4100 | tf_op jit(solution)/shard_map/scatter-add | solution.py:121
  172.0 13.6 %psum.39 = f32[1024]{0:T(1024)S(1)} all-reduce(f32[1024]{0:T(1024)S(1)} %scatter_custom_fusion.9), channel_id=1, replica_groups=mesh['col'=4,'wide'=8] {'wide'}, use_global_device_ids=true, to_apply=%region_20.23 | all-reduce | flops 1024 | bytes 8192 | tf_op jit(solution)/shard_map/psum | solution.py:121
  185.6 7.5 %all_gather.15 = bf16[4096]{0:T(1024)(128)(2,1)S(1)} all-gather(bf16[1024]{0:T(1024)(128)(2,1)S(1)} %get-tuple-element.8), channel_id=1, replica_groups=mesh['col'=4,'wide'=8] {'col'}, dimensions={0}, use_global_device_ids=true | all-gather | bytes 10240 | tf_op jit(solution)/shard_map/all_gather | solution.py:123
  193.1 1.9 gather_fusion.2
  195.1 0.4 fusion.39
  195.5 0.6 copy.52
  196.2 0.6 dynamic_slice.3
  (44 shorter events, 1.2 us)
Async XLA Ops:
  0.6 7.3 %copy-start = (bf16[16,320,128]{2,1,0:T(8,128)(2,1)S(1)}, bf16[16,320,128]{2,1,0:T(8,128)(2,1)}, u32[]{:S(2)}) copy-start(bf16[16,320,128]{2,1,0:T(8,128)(2,1)} %param.14) | copy-start | bytes 3932164
  8.9 2.2 %copy-start.3 = (f32[24]{0:T(128)S(1)}, f32[24]{0:T(128)}, u32[]{:S(2)}) copy-start(f32[24]{0:T(128)} %param.13) | copy-start | bytes 292
  21.9 13.8 %copy-start.1 = (bf16[2,2560]{1,0:T(2,128)(2,1)S(1)}, bf16[2,2560]{1,0:T(2,128)(2,1)}, u32[]{:S(2)}) copy-start(bf16[2,2560]{1,0:T(2,128)(2,1)} %param.15) | copy-start | bytes 30724
  21.9 14.1 %copy-start.2 = (s32[2]{0:T(128)S(1)}, s32[2]{0:T(128)}, u32[]{:S(2)}) copy-start(s32[2]{0:T(128)} %param.19) | copy-start | bytes 28
  30.6 9.7 %all-to-all-start.2 = ((f32[4,64,1]{1,2,0:T(1,128)}), f32[4,64,1]{1,2,0:T(1,128)S(1)}, u32[]{:S(2)}, u32[]{:S(2)}) async-start(f32[4,64,1]{1,2,0:T(1,128)} %bitcast.25), calls=%async_computation.2 | async-start | bytes 4096 | tf_op jit(solution)/shard_map/all_to_all | solution.py:95
  40.2 9.3 %all-to-all-start = ((s32[4,64,1]{1,2,0:T(1,128)}), s32[4,64,1]{1,2,0:T(1,128)S(1)}, u32[]{:S(2)}, u32[]{:S(2)}) async-start(s32[4,64,1]{1,2,0:T(1,128)} %bitcast.9), calls=%async_computation | async-start | bytes 4096 | tf_op jit(solution)/shard_map/all_to_all | solution.py:96
  49.5 8.8 %all-to-all-start.1 = ((f32[4,64,1]{1,2,0:T(1,128)}), f32[4,64,1]{1,2,0:T(1,128)S(1)}, u32[]{:S(2)}, u32[]{:S(2)}) async-start(f32[4,64,1]{1,2,0:T(1,128)} %bitcast.15), calls=%async_computation.1 | async-start | bytes 4096 | tf_op jit(solution)/shard_map/all_to_all | solution.py:94
  58.9 31.1 %all-to-all-start.5 = ((s32[4,2,128]{2,1,0:T(2,128)}), s32[4,2,128]{2,1,0:T(2,128)S(1)}, u32[]{:S(2)}, u32[]{:S(2)}) async-start(s32[4,2,128]{2,1,0:T(2,128)} %broadcast_in_dim.82), calls=%async_computation.5 | async-start | bytes 8192 | tf_op jit(solution)/shard_map/all_to_all | solution.py:98
  90.1 9.4 %all-to-all-start.3 = ((s32[4,64,1]{1,2,0:T(1,128)}), s32[4,64,1]{1,2,0:T(1,128)S(1)}, u32[]{:S(2)}, u32[]{:S(2)}) async-start(s32[4,64,1]{1,2,0:T(1,128)} %all_to_all.48), calls=%async_computation.3 | async-start | bytes 4096 | tf_op jit(solution)/shard_map/all_to_all | solution.py:97
  99.5 9.2 %all-to-all-start.4 = ((f32[4,64,128]{2,1,0:T(8,128)}), f32[4,64,128]{2,1,0:T(8,128)S(1)}, u32[]{:S(2)}, u32[]{:S(2)}) async-start(f32[4,64,128]{2,1,0:T(8,128)} %bitcast.28), calls=%async_computation.4 | async-start | bytes 262144 | tf_op jit(solution)/shard_map/all_to_all | solution.py:93
where the time goes:
time: 198 us; the launch traced here: 197 us
  blocking collectives  86.3 us (44%)
  local copies, waits for them, and re-layouts  45.9 us (23%)
  starting transfers between devices  23.3 us (12%)
  other arithmetic  18.9 us (10%)
  matrix products  12.2 us (6%)
  waiting for transfers between devices  9.18 us (5%)
    psum x3, blocking collectives, body(): lax.psum(jax.ops.segment_sum(row_value, recv_row, num_segments=per_col),...  40.8 us
    all_gather x3, blocking collectives, body(): solution_all = lax.all_gather(col_part, 'col', axis=0, tiled=True)  24.2 us
    gather x3, local copies, waits for them, and re-layouts, body(): jnp.take(solution_all, recv_cols).reshape(col_count, sub_count, prim_count)  18.4 us
    psum x1, blocking collectives, body(): col_load, col_diag = lax.psum((block_load, block_diag), 'wide')  13.8 us
    all_gather x1, blocking collectives, body(): lax.all_gather(col_part.astype(jnp.bfloat16), 'col', axis=0, tiled=True)  7.46 us
    scatter-add x3, other arithmetic, body(): jax.ops.segment_sum(row_value, recv_row, num_segments=per_col)  6.97 us
    dot_general x1, matrix products, body(): jnp.einsum('fij,fjp->fip', flux_jac, paired, preferred_element_type=jnp.f...  6.02 us
    all_to_all x1, starting transfers between devices, body(): lax.all_to_all(send_diag, 'col', split_axis=0, concat_axis=0, tiled=True)  5.17 us
  transfers between devices with their start and end apart: 6, of which 3 were waited for; matrix products, arithmetic and copies ran while one was open for 10% of the time, Pallas kernels for 0%

commit v1 on v0

v1 whole, which is shorter than its diff:
```python
import functools

import jax
import jax.numpy as jnp
from jax import lax
from jax.experimental import pallas as pl
from jax.experimental.pallas import tpu as pltpu
from jax.sharding import PartitionSpec as P

ITERS = 3
damping = 0.7
F32 = jnp.float32
BF16 = jnp.bfloat16
MESH = pl.DeviceIdType.MESH


def split2(value):
    high = value.astype(BF16)
    return high, (value - high.astype(F32)).astype(BF16)


def dot(lhs, rhs):
    return jnp.dot(lhs, rhs, preferred_element_type=F32)


def onehot_dot(onehot, value):
    width = value.shape[1]
    both = dot(onehot, jnp.concatenate(split2(value), axis=1))
    return both[:, :width] + both[:, width:]


def column(row, size):
    return jnp.transpose(jnp.broadcast_to(row, (size, size)))


def pick_row(value, row):
    return jnp.sum(jnp.where(iota(value.shape, 0) == row, value, 0.0), axis=0, keepdims=True)


def iota(shape, axis):
    return lax.broadcasted_iota(jnp.int32, shape, axis)


def local_kernel(
    dims, faces_ref, diss_ref, counts_ref, flux_ref, basis_ref, res_ref, primal_ref, owner_ref,
    schur_ref, load_ref, high_ref, low_ref, image,
):
    step_faces, steps_sub, elem_sub, units, prim = dims
    step = pl.program_id(0)
    sub = step // steps_sub
    part = step % steps_sub

    @pl.when(part == 0)
    def _():
        image[...] = jnp.zeros_like(image)

    for k in range(step_faces):
        face = step * step_faces + k
        first = faces_ref[face, 0]
        second = faces_ref[face, 1]
        basis_a = basis_ref[sub * elem_sub + first].astype(F32)
        basis_b = basis_ref[sub * elem_sub + second].astype(F32)
        flux = dot(flux_ref[k], (basis_a + basis_b).astype(BF16))
        image[first] += 0.5 * flux + (0.5 * diss_ref[face]) * (basis_a - basis_b)

    @pl.when(part == steps_sub - 1)
    def _():
        alive_col = (iota((prim, prim), 0) < counts_ref[sub]).astype(F32)
        alive_row = (iota((prim, prim), 1) < counts_ref[sub]).astype(F32)
        flat = basis_ref[pl.ds(sub * elem_sub, elem_sub)].reshape(elem_sub * units, prim)
        img = image[...].reshape(elem_sub * units, prim).astype(BF16)
        schur = lax.dot_general(flat, img, (((0,), (0,)), ((), ())), preferred_element_type=F32)
        schur_ref[...] = schur * alive_col * alive_row
        residual = pick_row(res_ref[...].astype(F32), sub).astype(BF16)
        load_ref[...] = column(dot(residual, flat), prim) * alive_col
        dof = column(pick_row(primal_ref[...].astype(F32), sub), prim).astype(jnp.int32)
        owner = owner_ref[...]
        rows = owner.shape[0]
        pick = ((dof[:, :1] >> 7) == iota((prim, rows), 1)).astype(F32).astype(BF16)
        table = jnp.concatenate(
            [(owner >> 7).astype(F32).astype(BF16), (owner & 127).astype(F32).astype(BF16)], axis=1
        )
        found = dot(pick, table)
        lane = ((dof & 127) == iota((prim, 128), 1)).astype(F32)
        high = jnp.sum(found[:, :128] * lane, axis=1, keepdims=True)
        low = jnp.sum(found[:, 128:] * lane, axis=1, keepdims=True)
        high_ref[...] = jnp.broadcast_to(high, (prim, 128))
        low_ref[...] = jnp.broadcast_to(low, (prim, 128))


def sweep_kernel(
    dims, counts_ref, schur_ref, load_ref, high_ref, low_ref, basis_ref,
    corr_ref, sol_ref, basis_buf, out0, in0, outs, ins, shares, mine, send_sem, recv_sem, copy_sem,
):
    col_count, wide_count, sub_count, prim = dims
    n = col_count * wide_count
    rows = sub_count * prim
    me = lax.axis_index("col") * wide_count + lax.axis_index("wide")

    def peer(k):
        to = lax.rem(me + k, n)
        return to, (to // wide_count, lax.rem(to, wide_count))

    barrier = pltpu.get_barrier_semaphore()

    @pl.loop(1, n)
    def _(k):
        pl.semaphore_signal(barrier, inc=1, device_id=peer(k)[1], device_id_type=MESH)

    fetch = pltpu.make_async_copy(basis_ref, basis_buf, copy_sem)
    fetch.start()

    schur_high, schur_low = split2(schur_ref[...])
    high = high_ref[...].astype(jnp.int32)
    low_hot = (low_ref[...].astype(jnp.int32) == iota((rows, 128), 1)).astype(F32)
    row_hot = (high[:, :1] == iota((rows, n), 1)).astype(F32).astype(BF16)
    hots = []
    for sub in range(sub_count):
        part = jnp.transpose(high_ref[pl.ds(sub * prim, prim), :])[:1, :].astype(jnp.int32)
        hots.append((jnp.broadcast_to(part, (n, prim)) == iota((n, prim), 0)).astype(F32).astype(BF16))
    row_hot_t = jnp.concatenate(hots, axis=1)

    diag = jnp.concatenate(
        [
            jnp.sum(
                schur_ref[pl.ds(sub * prim, prim), :]
                * (iota((prim, prim), 0) == iota((prim, prim), 1)).astype(F32),
                axis=1, keepdims=True,
            )
            for sub in range(sub_count)
        ],
        axis=0,
    )
    start = onehot_dot(
        row_hot_t, jnp.concatenate([load_ref[...] * low_hot, diag * low_hot], axis=1)
    )
    out0[...] = start.reshape(n, 1, 256)
    pl.semaphore_wait(barrier, n - 1)

    def scatter_out(source, target, hop):
        @pl.loop(1, n)
        def _(k):
            to, where = peer(k)
            pltpu.make_async_remote_copy(
                src_ref=source.at[to], dst_ref=target.at[me],
                send_sem=send_sem.at[hop], recv_sem=recv_sem.at[hop],
                device_id=where, device_id_type=MESH,
            ).start()

        target[me] = source[me]

    def arrived(target, hop):
        some = target.at[pl.ds(0, n - 1)]
        pltpu.make_async_copy(some, some, recv_sem.at[hop]).wait()

    def left(target, hop):
        some = target.at[pl.ds(0, n - 1)]
        pltpu.make_async_copy(some, some, send_sem.at[hop]).wait()

    def share(value, rnd):
        mine[rnd] = value

        @pl.loop(1, n)
        def _(k):
            to, where = peer(k)
            pltpu.make_async_remote_copy(
                src_ref=mine.at[rnd], dst_ref=shares.at[rnd, me],
                send_sem=send_sem.at[2 * rnd + 1], recv_sem=recv_sem.at[2 * rnd + 1],
                device_id=where, device_id_type=MESH,
            ).start()

        shares[rnd, me] = value
        arrived(shares.at[rnd], 2 * rnd + 1)
        whole = shares[rnd].reshape(n, 128)
        return onehot_dot(row_hot, whole) * low_hot

    scatter_out(out0, in0, 0)
    arrived(in0, 0)
    total = jnp.sum(in0[...], axis=0)
    load_own = total[:, :128]
    scale = damping / jnp.maximum(total[:, 128:], 1.0)
    current = load_own * scale
    for rnd in range(ITERS):
        spread = share(current, rnd)
        sp_high, sp_low = split2(spread)
        prods = []
        for sub in range(sub_count):
            part = slice(sub * prim, (sub + 1) * prim)
            both = dot(schur_high[part], jnp.concatenate([sp_high[part], sp_low[part]], axis=1))
            prods.append(both[:, :128] + both[:, 128:] + dot(schur_low[part], sp_high[part]))
        row_value = jnp.sum(jnp.concatenate(prods, axis=0), axis=1, keepdims=True)
        outs[rnd] = onehot_dot(row_hot_t, row_value * low_hot).reshape(n, 1, 128)
        scatter_out(outs.at[rnd], ins.at[rnd], 2 * rnd + 2)
        arrived(ins.at[rnd], 2 * rnd + 2)
        current = current + (load_own - jnp.sum(ins[rnd], axis=0)) * scale
    sol_ref[...] = current
    near = jnp.sum(share(current, ITERS), axis=1, keepdims=True)
    fetch.wait()
    for sub in range(sub_count):
        near_sub = jnp.broadcast_to(near[sub * prim:(sub + 1) * prim], (prim, prim))
        alive = (iota((prim, prim), 0) < counts_ref[sub]).astype(F32)
        near_row = jnp.transpose(near_sub * alive)[:16].astype(BF16)
        found = lax.dot_general(
            near_row, basis_buf[sub], (((1,), (1,)), ((), ())), preferred_element_type=F32
        )
        corr_ref[pl.ds(sub, 1), :] = found[:1]
    left(in0, 0)
    for rnd in range(ITERS + 1):
        left(shares.at[rnd], 2 * rnd + 1)
    for rnd in range(ITERS):
        left(ins.at[rnd], 2 * rnd + 2)


def body(flux_jac, dissipation, basis, residual, face_elems, primal, coarse_owner, counts):
    col_count = lax.axis_size("col")
    wide_count = lax.axis_size("wide")
    n = col_count * wide_count
    sub_count = residual.shape[0]
    face_count = flux_jac.shape[0]
    elem_sub = basis.shape[0] // sub_count
    units, prim = basis.shape[1:]
    rows = sub_count * prim
    step_faces = 4
    steps = face_count // step_faces
    steps_sub = steps // sub_count
    smem = pl.BlockSpec(memory_space=pltpu.SMEM)
    vmem = pl.BlockSpec(memory_space=pltpu.VMEM)
    block = pl.BlockSpec((prim, 128), lambda i: (i // steps_sub, 0))
    schur, load, high, low = pl.pallas_call(
        functools.partial(local_kernel, (step_faces, steps_sub, elem_sub, units, prim)),
        grid=(steps,),
        in_specs=[
            smem, smem, smem,
            pl.BlockSpec((step_faces, units, units), lambda i: (i, 0, 0)),
            vmem, vmem, vmem, vmem,
        ],
        out_specs=[block] * 4,
        out_shape=[jax.ShapeDtypeStruct((rows, 128), F32)] * 4,
        scratch_shapes=[pltpu.VMEM((elem_sub, units, prim), F32)],
        compiler_params=pltpu.CompilerParams(vmem_limit_bytes=32 << 20),
        name="local",
    )(face_elems, dissipation, counts, flux_jac, basis, residual, primal,
      coarse_owner.reshape(-1, 128))
    basis_sub = basis.reshape(sub_count, elem_sub * units, prim)
    correction, own = pl.pallas_call(
        functools.partial(sweep_kernel, (col_count, wide_count, sub_count, prim)),
        in_specs=[smem, vmem, vmem, vmem, vmem, pl.BlockSpec(memory_space=pl.ANY)],
        out_specs=[vmem, vmem],
        out_shape=[
            jax.ShapeDtypeStruct(residual.shape, F32),
            jax.ShapeDtypeStruct((1, 128), F32),
        ],
        scratch_shapes=[
            pltpu.VMEM(basis_sub.shape, BF16),
            pltpu.VMEM((n, 1, 256), F32),
            pltpu.VMEM((n, 1, 256), F32),
            pltpu.VMEM((ITERS, n, 1, 128), F32),
            pltpu.VMEM((ITERS, n, 1, 128), F32),
            pltpu.VMEM((ITERS + 1, n, 1, 128), F32),
            pltpu.VMEM((ITERS + 1, 1, 128), F32),
            pltpu.SemaphoreType.DMA((2 * ITERS + 2,)),
            pltpu.SemaphoreType.DMA((2 * ITERS + 2,)),
            pltpu.SemaphoreType.DMA,
        ],
        compiler_params=pltpu.CompilerParams(
            collective_id=0, has_side_effects=True, vmem_limit_bytes=32 << 20
        ),
        name="sweeps",
    )(counts, schur, load, high, low, basis_sub)
    return correction, own.reshape(128)


def solution(mesh):
    return jax.shard_map(
        body,
        mesh=mesh,
        in_specs=(
            P(("col", "wide"), None, None),
            P(("col", "wide")),
            P(("col", "wide"), None, None),
            P(("col", "wide"), None),
            P(("col", "wide"), None),
            P(("col", "wide"), None),
            P(),
            P(("col", "wide")),
        ),
        out_specs=(P(("col", "wide"), None), P(("col", "wide"))),
        check_vma=False,
    )
```

time: 198 us -> 62.4 us (0.32)
  blocking collectives: 86.3 us -> 0 us
  Pallas kernels: 0 us -> 52.1 us
  local copies, waits for them, and re-layouts: 45.9 us -> 9.27 us
  starting transfers between devices: 23.3 us -> 0 us
  other arithmetic: 18.9 us -> 0 us
  matrix products: 12.2 us -> 0 us
  waiting for transfers between devices: 9.18 us -> 0 us
    psum x4 -> x0, blocking collectives: 54.6 us -> none  [the longest x3 40.8 us: body(): lax.psum(jax.ops.segment_sum(row_value, recv_row, num_segments=per_col),...]
    pallas_call x0 -> x2, Pallas kernels: none -> 52.1 us  [the longest x1 47.2 us: body(): pl.pallas_call(functools.partial(sweep_kernel, (col_count, wide_count, su...]
    all_gather x4 -> x0, blocking collectives: 31.6 us -> none  [the longest x3 24.2 us: body(): solution_all = lax.all_gather(col_part, 'col', axis=0, tiled=True)]
    gather x9 -> x0, local copies, waits for them, and re-layouts: 27.2 us -> none  [the longest x3 18.4 us: body(): jnp.take(solution_all, recv_cols).reshape(col_count, sub_count, prim_count)]
    all_to_all x6 -> x0, starting transfers between devices: 23.3 us -> none  [the longest x1 5.17 us: body(): lax.all_to_all(send_diag, 'col', split_axis=0, concat_axis=0, tiled=True)]
    dot_general x8 -> x0, matrix products: 12.2 us -> none  [the longest x1 6.02 us: body(): jnp.einsum('fij,fjp->fip', flux_jac, paired, preferred_element_type=jnp.f...]
    scatter-add x5 -> x0, other arithmetic: 11.6 us -> none  [the longest x3 6.97 us: body(): jax.ops.segment_sum(row_value, recv_row, num_segments=per_col)]
    unnamed x8 -> x17, local copies, waits for them, and re-layouts: 0.03 us -> 9.27 us
  transfers between devices with their start and end apart: 6 -> 0, of which waited for: 3 -> 0; matrix products, arithmetic and copies ran while one was open for 10% -> 0% of each run, Pallas kernels for 0% -> 0%
where the time goes in v1:
time: 62.4 us; the launch traced here: 62.1 us
  Pallas kernels  52.1 us (83%)
  local copies, waits for them, and re-layouts  9.27 us (15%)
  between operations  0.65 us (1%)
    pallas_call x1, Pallas kernels, body(): pl.pallas_call(functools.partial(sweep_kernel, (col_count, wide_count, su...  47.2 us
    unnamed x17, local copies, waits for them, and re-layouts  9.27 us
    pallas_call x1, Pallas kernels, body(): pl.pallas_call(functools.partial(local_kernel, (step_faces, steps_sub, el...  4.97 us

profile of v1, /device:TPU:0, one launch (start us, length us, event | category | flops | bytes accessed | tf_op | source)
XLA Modules:
  0.0 62.1 jit_solution(4994554449898583115)
XLA Ops:
  0.6 0.8 %copy.10.faces_ref = s32[24,2]{1,0:T(8,128)S(1)} copy(s32[24,2]{0,1:T(2,128)} %param.12) | data formatting | bytes 384 | tf_op args[4]
  1.4 0.0 copy-start
  1.4 2.7 %copy-done = bf16[24,320,320]{2,1,0:T(8,128)(2,1)S(1)} copy-done((bf16[24,320,320]{2,1,0:T(8,128)(2,1)S(1)}, bf16[24,320,320]{2,1,0:T(8,128)(2,1)}, u32[]{:S(2)}) %copy-start) | copy-done | bytes 4915224
  4.1 0.0 copy-start.1
  4.1 1.3 %copy-done.1 = bf16[16,320,128]{2,1,0:T(8,128)(2,1)S(1)} copy-done((bf16[16,320,128]{2,1,0:T(8,128)(2,1)S(1)}, bf16[16,320,128]{2,1,0:T(8,128)(2,1)}, u32[]{:S(2)}) %copy-start.1) | copy-done | bytes 1310744
  5.4 0.0 copy-start.2
  5.4 0.7 %copy-done.2 = s32[4096]{0:T(1024)S(1)} copy-done((s32[4096]{0:T(1024)S(1)}, s32[4096]{0:T(1024)}, u32[]{:S(2)}) %copy-start.2) | copy-done | bytes 16408
  6.1 0.0 copy-start.3
  6.1 0.7 %copy-done.3 = bf16[2,2560]{1,0:T(2,128)(2,1)S(1)} copy-done((bf16[2,2560]{1,0:T(2,128)(2,1)S(1)}, bf16[2,2560]{1,0:T(2,128)(2,1)}, u32[]{:S(2)}) %copy-start.3) | copy-done | bytes 10264
  6.8 0.0 copy-start.4
  6.8 0.7 %copy-done.4 = s32[2]{0:T(128)S(1)} copy-done((s32[2]{0:T(128)S(1)}, s32[2]{0:T(128)}, u32[]{:S(2)}) %copy-start.4) | copy-done | bytes 32
  7.5 0.0 copy-start.5
  7.5 0.7 %copy-done.5 = s32[2,128]{1,0:T(2,128)S(1)} copy-done((s32[2,128]{1,0:T(2,128)S(1)}, s32[2,128]{1,0:T(2,128)}, u32[]{:S(2)}) %copy-start.5) | copy-done | bytes 1048
  8.1 0.0 copy-start.6
  8.1 0.7 %copy-done.6 = f32[24]{0:T(128)S(1)} copy-done((f32[24]{0:T(128)S(1)}, f32[24]{0:T(128)}, u32[]{:S(2)}) %copy-start.6) | copy-done | bytes 120
  8.8 5.0 %local.1 = (f32[256,128]{1,0:T(8,128)S(1)}, f32[256,128]{1,0:T(8,128)S(1)}, f32[256,128]{1,0:T(8,128)S(1)}, f32[256,128]{1,0:T(8,128)S(1)}) custom-call(s32[24,2]{1,0:T(8,128)S(1)} %copy.10.faces_ref, f32[24]{0:T(128)S(1)} %copy-done.6, s32[2]{0:T(128)S(1)} %copy-done.4, bf16[24,320,320]{2,1,0:T(8,128)(2,1)S(1)} %copy-done, ...), custom_call_target="tpu_custom_call" | custom-call | tf_op jit(solution)/shard_map/local/pallas_call | solution.py:229
  13.8 47.2 %sweeps.1 = (f32[2,2560]{1,0:T(2,128)S(1)}, f32[1,128]{1,0:T(1,128)S(1)}) custom-call(s32[2]{0:T(128)S(1)} %copy-done.4, f32[256,128]{1,0:T(8,128)S(1)} %get-tuple-element.8.schur_ref, f32[256,128]{1,0:T(8,128)S(1)} %get-tuple-element.9.load_ref, f32[256,128]{1,0:T(8,128)S(1)} %get-tuple-element.10.high_ref, f32[256,128]{1,0:T(8,128)S(1)} %get-tuple-element.11.low_ref, ...), custom_call_target="tpu_custom_call" | custom-call | tf_op jit(solution)/shard_map/sweeps/pallas_call | solution.py:245
  60.9 0.6 copy.13
  61.6 0.5 copy.14
Async XLA Ops:
  1.4 2.7 %copy-start = (bf16[24,320,320]{2,1,0:T(8,128)(2,1)S(1)}, bf16[24,320,320]{2,1,0:T(8,128)(2,1)}, u32[]{:S(2)}) copy-start(bf16[24,320,320]{2,1,0:T(8,128)(2,1)} %flux_ref.1) | copy-start | bytes 14745604
  4.1 1.3 %copy-start.1 = (bf16[16,320,128]{2,1,0:T(8,128)(2,1)S(1)}, bf16[16,320,128]{2,1,0:T(8,128)(2,1)}, u32[]{:S(2)}) copy-start(bf16[16,320,128]{2,1,0:T(8,128)(2,1)} %basis_ref.1) | copy-start | bytes 3932164
  5.4 0.7 %copy-start.2 = (s32[4096]{0:T(1024)S(1)}, s32[4096]{0:T(1024)}, u32[]{:S(2)}) copy-start(s32[4096]{0:T(1024)} %param.14) | copy-start | bytes 49156
  6.1 0.7 %copy-start.3 = (bf16[2,2560]{1,0:T(2,128)(2,1)S(1)}, bf16[2,2560]{1,0:T(2,128)(2,1)}, u32[]{:S(2)}) copy-start(bf16[2,2560]{1,0:T(2,128)(2,1)} %res_ref.1) | copy-start | bytes 30724
  6.8 0.7 %copy-start.4 = (s32[2]{0:T(128)S(1)}, s32[2]{0:T(128)}, u32[]{:S(2)}) copy-start(s32[2]{0:T(128)} %counts_ref.3) | copy-start | bytes 28
  7.5 0.7 %copy-start.5 = (s32[2,128]{1,0:T(2,128)S(1)}, s32[2,128]{1,0:T(2,128)}, u32[]{:S(2)}) copy-start(s32[2,128]{1,0:T(2,128)} %primal_ref.1) | copy-start | bytes 3076
  8.1 0.7 %copy-start.6 = (f32[24]{0:T(128)S(1)}, f32[24]{0:T(128)}, u32[]{:S(2)}) copy-start(f32[24]{0:T(128)} %diss_ref.1) | copy-start | bytes 292

commit v2 on v0

v2 whole, which is shorter than its diff:
```python
import functools

import jax
import jax.numpy as jnp
from jax import lax
from jax.experimental import pallas as pl
from jax.experimental.pallas import tpu as pltpu
from jax.sharding import PartitionSpec as P

ITERS = 3
damping = 0.7
F32 = jnp.float32
BF16 = jnp.bfloat16
MESH = pl.DeviceIdType.MESH
UNROLL = 8


def split2(value):
    high = value.astype(BF16)
    return high, (value - high.astype(F32)).astype(BF16)


def dot(lhs, rhs, left=1, right=0):
    return lax.dot_general(lhs, rhs, (((left,), (right,)), ((), ())), preferred_element_type=F32)


def iota(shape, axis):
    return lax.broadcasted_iota(jnp.int32, shape, axis)


def hot(row, size):
    return (jnp.broadcast_to(row, (size, row.shape[1])) == iota((size, row.shape[1]), 0)).astype(F32)


def rows_sum(value):
    return jnp.sum(value, axis=0, keepdims=True)


def each(first, last, act):
    if last - first <= UNROLL:
        for k in range(first, last):
            act(k)
    else:
        pl.loop(first, last)(act)


def kernel(
    dims, faces_ref, diss_ref, counts_ref, res_ref, primal_ref, owner_ref, flux_ref, basis_ref,
    corr_ref, sol_ref, flux_buf, basis_buf, info_own, info, row_own, rows, hots, lows,
    dense0, denses, send_sem, recv_sem, flux_sem, basis_sem,
):
    col_count, wide_count, sub_count, face_sub, elem_sub, units, prim, chunk = dims
    n = col_count * wide_count
    my_col, my_wide = lax.axis_index("col"), lax.axis_index("wide")

    def wide_peer(k):
        return (my_col, lax.rem(my_wide + k, wide_count))

    def col_peer(k):
        return (lax.rem(my_col + k, col_count), my_wide)

    faces = sub_count * face_sub
    loads = [
        pltpu.make_async_copy(
            flux_ref.at[pl.ds(i * chunk, chunk)], flux_buf.at[pl.ds(i * chunk, chunk)], flux_sem.at[i]
        )
        for i in range(faces // chunk)
    ]
    fetch = pltpu.make_async_copy(basis_ref, basis_buf, basis_sem)
    fetch.start()
    for copy in loads:
        copy.start()

    barrier = pltpu.get_barrier_semaphore()

    def greet(peer):
        def act(k):
            pl.semaphore_signal(barrier, inc=1, device_id=peer(k), device_id_type=MESH)
        return act

    each(1, wide_count, greet(wide_peer))
    each(1, col_count, greet(col_peer))

    owner = owner_ref[...]
    table = jnp.concatenate(
        [(owner >> 7).astype(F32).astype(BF16), (owner & 127).astype(F32).astype(BF16)], axis=1
    )
    highs_f, lows_f = [], []
    for sub in range(sub_count):
        dof = primal_ref[sub:sub + 1, :]
        found = dot(table, hot(dof >> 7, owner.shape[0]).astype(BF16), 0, 0)
        lane = hot(dof & 127, 128)
        highs_f.append(rows_sum(found[:128] * lane))
        lows_f.append(rows_sum(found[128:] * lane))

    fetch.wait()
    schurs, load_rows, diag_rows, alive_rows = [], [], [], []
    for sub in range(sub_count):
        alive_col = (iota((prim, prim), 0) < counts_ref[sub]).astype(F32)
        alive_row = (iota((prim, prim), 1) < counts_ref[sub]).astype(F32)
        schur = jnp.zeros((prim, prim), F32)
        for k in range(face_sub):
            face = sub * face_sub + k
            if face % chunk == 0:
                loads[face // chunk].wait()
            basis_first = basis_buf[sub * elem_sub + faces_ref[0, face]]
            basis_a = basis_first.astype(F32)
            basis_b = basis_buf[sub * elem_sub + faces_ref[1, face]].astype(F32)
            flux = dot(flux_buf[face], (basis_a + basis_b).astype(BF16))
            image = 0.5 * flux + (0.5 * diss_ref[face]) * (basis_a - basis_b)
            schur = schur + dot(basis_first, image.astype(BF16), 0, 0)
        schur = schur * alive_col * alive_row
        flat = basis_buf[sub * elem_sub:(sub + 1) * elem_sub].reshape(elem_sub * units, prim)
        load_rows.append(dot(res_ref[sub:sub + 1, :], flat) * alive_row[:1])
        diag_rows.append(
            rows_sum(schur * (iota((prim, prim), 0) == iota((prim, prim), 1)).astype(F32))
        )
        alive_rows.append(alive_row[:1])
        high, low = split2(schur)
        schurs.append(jnp.concatenate([high, high, low], axis=1))

    info_own[...] = jnp.concatenate(
        [jnp.concatenate(part, axis=1) for part in (load_rows, diag_rows, highs_f, lows_f)], axis=0
    )
    pl.semaphore_wait(barrier, wide_count + col_count - 2)

    def send(source, target, peer, index, count, hop):
        def act(k):
            pltpu.make_async_remote_copy(
                src_ref=source, dst_ref=target.at[index],
                send_sem=send_sem.at[hop], recv_sem=recv_sem.at[hop],
                device_id=peer(k), device_id_type=MESH,
            ).start()

        each(1, count, act)

    def wait(target, count, sem):
        some = target.at[pl.ds(0, count - 1)]
        pltpu.make_async_copy(some, some, sem).wait()

    def to_dense(value_of, parts):
        def add(w, total):
            pieces = [
                piece
                for value in value_of(w)
                for piece in split2(jnp.broadcast_to(value, (n, value.shape[1])) * hots[w].astype(F32))
            ]
            return total + dot(jnp.concatenate(pieces, axis=0), lows[w], 1, 1)

        total = jnp.zeros((2 * parts * n, 128), F32)
        if wide_count <= UNROLL:
            for w in range(wide_count):
                total = add(w, total)
        else:
            total = lax.fori_loop(0, wide_count, add, total)
        return jnp.concatenate(
            [total[2 * i * n:(2 * i + 1) * n] + total[(2 * i + 1) * n:(2 * i + 2) * n] for i in range(parts)],
            axis=0,
        )

    def col_sum(value, target, hop):
        target[my_col] = value
        send(target.at[my_col], target, col_peer, my_col, col_count, hop)
        wait(target, col_count, recv_sem.at[hop])
        total = target[0]
        for c in range(1, col_count):
            total = total + target[c]
        return total

    info[my_wide] = info_own[...]
    send(info_own, info, wide_peer, my_wide, wide_count, 0)
    wait(info, wide_count, recv_sem.at[0])

    def prepare(w):
        hots[w] = hot(info[w, 2:3, :].astype(jnp.int32), n).astype(BF16)
        lows[w] = hot(info[w, 3:4, :].astype(jnp.int32), 128).astype(BF16)

    each(0, wide_count, prepare)
    total = col_sum(
        to_dense(lambda w: [info[w, 0:1, :], info[w, 1:2, :]], 2), dense0, 1
    )
    load = total[:n]
    scale = damping / jnp.maximum(total[n:], 1.0)
    current = load * scale
    my_hot = hot(jnp.concatenate(highs_f, axis=1).astype(jnp.int32), n).astype(BF16)
    my_hot = jnp.concatenate([my_hot, my_hot], axis=0)
    my_low = hot(jnp.concatenate(lows_f, axis=1).astype(jnp.int32), 128)

    def gather(vector):
        return rows_sum(dot(jnp.concatenate(split2(vector), axis=0), my_hot, 0, 0) * my_low)

    for rnd in range(ITERS):
        high, low = split2(gather(current))
        prods = []
        for sub in range(sub_count):
            part = slice(sub * prim, (sub + 1) * prim)
            values = jnp.concatenate([high[:, part], low[:, part], high[:, part]], axis=1)
            prods.append(dot(values, schurs[sub], 1, 1))
        row_own[rnd] = jnp.concatenate(prods, axis=1)
        rows[rnd, my_wide] = row_own[rnd]
        send(row_own.at[rnd], rows.at[rnd], wide_peer, my_wide, wide_count, 2 * rnd + 2)
        wait(rows.at[rnd], wide_count, recv_sem.at[2 * rnd + 2])
        total = col_sum(to_dense(lambda w: [rows[rnd, w]], 1), denses.at[rnd], 2 * rnd + 3)
        current = current + (load - total) * scale

    sol_ref[...] = rows_sum(
        jnp.where(iota((n, 128), 0) == my_col * wide_count + my_wide, current, 0.0)
    )
    near = gather(current)
    for sub in range(sub_count):
        near_sub = (near[:, sub * prim:(sub + 1) * prim] * alive_rows[sub]).astype(BF16)
        flat = basis_buf[sub * elem_sub:(sub + 1) * elem_sub].reshape(elem_sub * units, prim)
        corr_ref[sub:sub + 1, :] = dot(near_sub, flat, 1, 1)

    wait(info, wide_count, send_sem.at[0])
    wait(dense0, col_count, send_sem.at[1])
    for rnd in range(ITERS):
        wait(rows.at[rnd], wide_count, send_sem.at[2 * rnd + 2])
        wait(denses.at[rnd], col_count, send_sem.at[2 * rnd + 3])


def body(flux_jac, dissipation, basis, residual, face_elems, primal, coarse_owner, counts):
    col_count = lax.axis_size("col")
    wide_count = lax.axis_size("wide")
    n = col_count * wide_count
    sub_count = residual.shape[0]
    face_count = flux_jac.shape[0]
    elem_sub = basis.shape[0] // sub_count
    units, prim = basis.shape[1:]
    row_count = sub_count * prim
    chunk = 4
    smem = pl.BlockSpec(memory_space=pltpu.SMEM)
    vmem = pl.BlockSpec(memory_space=pltpu.VMEM)
    hbm = pl.BlockSpec(memory_space=pltpu.HBM)
    hops = 2 * ITERS + 2
    correction, own = pl.pallas_call(
        functools.partial(
            kernel,
            (col_count, wide_count, sub_count, face_count // sub_count, elem_sub, units, prim, chunk),
        ),
        in_specs=[smem, smem, smem, vmem, vmem, vmem, hbm, hbm],
        out_specs=[vmem, vmem],
        out_shape=[
            jax.ShapeDtypeStruct(residual.shape, F32),
            jax.ShapeDtypeStruct((1, 128), F32),
        ],
        scratch_shapes=[
            pltpu.VMEM(flux_jac.shape, BF16),
            pltpu.VMEM(basis.shape, BF16),
            pltpu.VMEM((4, row_count), F32),
            pltpu.VMEM((wide_count, 4, row_count), F32),
            pltpu.VMEM((ITERS, 1, row_count), F32),
            pltpu.VMEM((ITERS, wide_count, 1, row_count), F32),
            pltpu.VMEM((wide_count, n, row_count), BF16),
            pltpu.VMEM((wide_count, 128, row_count), BF16),
            pltpu.VMEM((col_count, 2 * n, 128), F32),
            pltpu.VMEM((ITERS, col_count, n, 128), F32),
            pltpu.SemaphoreType.DMA((hops,)),
            pltpu.SemaphoreType.DMA((hops,)),
            pltpu.SemaphoreType.DMA((face_count // chunk,)),
            pltpu.SemaphoreType.DMA,
        ],
        compiler_params=pltpu.CompilerParams(
            collective_id=0, has_side_effects=True, vmem_limit_bytes=48 << 20
        ),
        name="coarse",
    )(face_elems.T, dissipation, counts, residual, primal, coarse_owner.reshape(-1, 128), flux_jac, basis)
    return correction, own.reshape(128)


def solution(mesh):
    return jax.shard_map(
        body,
        mesh=mesh,
        in_specs=(
            P(("col", "wide"), None, None),
            P(("col", "wide")),
            P(("col", "wide"), None, None),
            P(("col", "wide"), None),
            P(("col", "wide"), None),
            P(("col", "wide"), None),
            P(),
            P(("col", "wide")),
        ),
        out_specs=(P(("col", "wide"), None), P(("col", "wide"))),
        check_vma=False,
    )
```

time: 198 us -> 49 us (0.25)
  blocking collectives: 86.3 us -> 0 us
  Pallas kernels: 0 us -> 41.5 us
  local copies, waits for them, and re-layouts: 45.9 us -> 6.51 us
  starting transfers between devices: 23.3 us -> 0 us
  other arithmetic: 18.9 us -> 0 us
  matrix products: 12.2 us -> 0 us
  waiting for transfers between devices: 9.18 us -> 0 us
    psum x4 -> x0, blocking collectives: 54.6 us -> none  [the longest x3 40.8 us: body(): lax.psum(jax.ops.segment_sum(row_value, recv_row, num_segments=per_col),...]
    pallas_call x0 -> x1, Pallas kernels: none -> 41.5 us  [body(): pl.pallas_call(functools.partial(kernel, (col_count, wide_count, sub_coun...]
    all_gather x4 -> x0, blocking collectives: 31.6 us -> none  [the longest x3 24.2 us: body(): solution_all = lax.all_gather(col_part, 'col', axis=0, tiled=True)]
    gather x9 -> x0, local copies, waits for them, and re-layouts: 27.2 us -> none  [the longest x3 18.4 us: body(): jnp.take(solution_all, recv_cols).reshape(col_count, sub_count, prim_count)]
    all_to_all x6 -> x0, starting transfers between devices: 23.3 us -> none  [the longest x1 5.17 us: body(): lax.all_to_all(send_diag, 'col', split_axis=0, concat_axis=0, tiled=True)]
    dot_general x8 -> x0, matrix products: 12.2 us -> none  [the longest x1 6.02 us: body(): jnp.einsum('fij,fjp->fip', flux_jac, paired, preferred_element_type=jnp.f...]
    scatter-add x5 -> x0, other arithmetic: 11.6 us -> none  [the longest x3 6.97 us: body(): jax.ops.segment_sum(row_value, recv_row, num_segments=per_col)]
    all_to_all x6 -> x0, waiting for transfers between devices: 9.18 us -> none  [the longest x1 5.01 us: body(): lax.all_to_all(send_vals, 'col', split_axis=0, concat_axis=0, tiled=True)]
  transfers between devices with their start and end apart: 6 -> 0, of which waited for: 3 -> 0; matrix products, arithmetic and copies ran while one was open for 10% -> 0% of each run, Pallas kernels for 0% -> 0%
where the time goes in v2:
time: 49 us; the launch traced here: 48.7 us
  Pallas kernels  41.5 us (85%)
  local copies, waits for them, and re-layouts  6.51 us (13%)
  between operations  0.66 us (1%)
    pallas_call x1, Pallas kernels, body(): pl.pallas_call(functools.partial(kernel, (col_count, wide_count, sub_coun...  41.5 us
    unnamed x16, local copies, waits for them, and re-layouts  6.51 us

profile of v2, /device:TPU:0, one launch (start us, length us, event | category | flops | bytes accessed | tf_op | source)
XLA Modules:
  0.0 48.7 jit_solution(4261221739331959684)
XLA Ops:
  0.6 0.0 copy-start
  0.6 1.3 %copy-done = bf16[16,320,128]{2,1,0:T(8,128)(2,1)S(1)} copy-done((bf16[16,320,128]{2,1,0:T(8,128)(2,1)S(1)}, bf16[16,320,128]{2,1,0:T(8,128)(2,1)}, u32[]{:S(2)}) %copy-start) | copy-done | bytes 1310744
  1.9 0.0 copy-start.1
  2.0 0.7 %copy-done.1 = s32[4096]{0:T(1024)S(1)} copy-done((s32[4096]{0:T(1024)S(1)}, s32[4096]{0:T(1024)}, u32[]{:S(2)}) %copy-start.1) | copy-done | bytes 16408
  2.7 0.0 copy-start.2
  2.7 0.7 %copy-done.2 = bf16[2,2560]{1,0:T(2,128)(2,1)S(1)} copy-done((bf16[2,2560]{1,0:T(2,128)(2,1)S(1)}, bf16[2,2560]{1,0:T(2,128)(2,1)}, u32[]{:S(2)}) %copy-start.2) | copy-done | bytes 10264
  3.4 0.0 copy-start.3
  3.4 0.7 %copy-done.3 = s32[24,2]{0,1:T(2,128)S(1)} copy-done((s32[24,2]{0,1:T(2,128)S(1)}, s32[24,2]{0,1:T(2,128)}, u32[]{:S(2)}) %copy-start.3) | copy-done | bytes 216
  4.0 0.0 copy-start.4
  4.1 0.7 %copy-done.4 = s32[2,128]{1,0:T(2,128)S(1)} copy-done((s32[2,128]{1,0:T(2,128)S(1)}, s32[2,128]{1,0:T(2,128)}, u32[]{:S(2)}) %copy-start.4) | copy-done | bytes 1048
  4.7 0.0 copy-start.5
  4.7 0.7 %copy-done.5 = f32[24]{0:T(128)S(1)} copy-done((f32[24]{0:T(128)S(1)}, f32[24]{0:T(128)}, u32[]{:S(2)}) %copy-start.5) | copy-done | bytes 120
  5.4 0.0 copy-start.6
  5.4 0.7 %copy-done.6 = s32[2]{0:T(128)S(1)} copy-done((s32[2]{0:T(128)S(1)}, s32[2]{0:T(128)}, u32[]{:S(2)}) %copy-start.6) | copy-done | bytes 32
  6.0 41.5 %coarse.1 = (f32[2,2560]{1,0:T(2,128)S(1)}, f32[1,128]{1,0:T(1,128)S(1)}) custom-call(s32[2,24]{1,0:T(2,128)S(1)} %bitcast.4, f32[24]{0:T(128)S(1)} %copy-done.5, s32[2]{0:T(128)S(1)} %copy-done.6, bf16[2,2560]{1,0:T(2,128)(2,1)S(1)} %copy-done.2, s32[2,128]{1,0:T(2,128)S(1)} %copy-done.4, s32[32,128]{1,0:T(8,128)S(1)} %bitcast.3, ...), custom_call_target="tpu_custom_call" | custom-call | tf_op jit(solution)/shard_map/coarse/pallas_call | solution.py:236
  47.6 0.6 %copy.12 = f32[2,2560]{1,0:T(2,128)} copy(f32[2,2560]{1,0:T(2,128)S(1)} %get-tuple-element.8) | data formatting | bytes 40960
  48.2 0.5 %copy.13 = f32[128]{0:T(128)} copy(f32[128]{0:T(128)S(1)} %bitcast.5) | data formatting | bytes 1024
Async XLA Ops:
  0.6 1.3 %copy-start = (bf16[16,320,128]{2,1,0:T(8,128)(2,1)S(1)}, bf16[16,320,128]{2,1,0:T(8,128)(2,1)}, u32[]{:S(2)}) copy-start(bf16[16,320,128]{2,1,0:T(8,128)(2,1)} %basis_ref.1) | copy-start | bytes 3932164
  1.9 0.7 %copy-start.1 = (s32[4096]{0:T(1024)S(1)}, s32[4096]{0:T(1024)}, u32[]{:S(2)}) copy-start(s32[4096]{0:T(1024)} %param.14) | copy-start | bytes 49156
  2.7 0.7 %copy-start.2 = (bf16[2,2560]{1,0:T(2,128)(2,1)S(1)}, bf16[2,2560]{1,0:T(2,128)(2,1)}, u32[]{:S(2)}) copy-start(bf16[2,2560]{1,0:T(2,128)(2,1)} %res_ref.1) | copy-start | bytes 30724
  3.4 0.7 %copy-start.3 = (s32[24,2]{0,1:T(2,128)S(1)}, s32[24,2]{0,1:T(2,128)}, u32[]{:S(2)}) copy-start(s32[24,2]{0,1:T(2,128)} %param.12) | copy-start | bytes 580
  4.0 0.7 %copy-start.4 = (s32[2,128]{1,0:T(2,128)S(1)}, s32[2,128]{1,0:T(2,128)}, u32[]{:S(2)}) copy-start(s32[2,128]{1,0:T(2,128)} %primal_ref.1) | copy-start | bytes 3076
  4.7 0.7 %copy-start.5 = (f32[24]{0:T(128)S(1)}, f32[24]{0:T(128)}, u32[]{:S(2)}) copy-start(f32[24]{0:T(128)} %diss_ref.1) | copy-start | bytes 292
  5.4 0.7 %copy-start.6 = (s32[2]{0:T(128)S(1)}, s32[2]{0:T(128)}, u32[]{:S(2)}) copy-start(s32[2]{0:T(128)} %counts_ref.1) | copy-start | bytes 28

commit v3 on v2

--- a/solution.py
+++ b/solution.py
@@ -12,7 +12,7 @@
 F32 = jnp.float32
 BF16 = jnp.bfloat16
 MESH = pl.DeviceIdType.MESH
-UNROLL = 8
+UNROLL = 16
 
 
 def split2(value):
@@ -52,12 +52,17 @@
     col_count, wide_count, sub_count, face_sub, elem_sub, units, prim, chunk = dims
     n = col_count * wide_count
     my_col, my_wide = lax.axis_index("col"), lax.axis_index("wide")
-
-    def wide_peer(k):
-        return (my_col, lax.rem(my_wide + k, wide_count))
-
-    def col_peer(k):
-        return (lax.rem(my_col + k, col_count), my_wide)
+    half = wide_count // 2
+    groups = col_count * half
+    core = lax.rem(my_wide, 2)
+    my_group = my_col * half + my_wide // 2
+
+    def group_peer(k):
+        to = lax.rem(my_group + groups - k, groups)
+        return (to // half, lax.rem(to, half) * 2 + core)
+
+    def core_peer(k):
+        return (my_col, my_wide + 1 - 2 * core)
 
     faces = sub_count * face_sub
     loads = [
@@ -78,8 +83,8 @@
             pl.semaphore_signal(barrier, inc=1, device_id=peer(k), device_id_type=MESH)
         return act
 
-    each(1, wide_count, greet(wide_peer))
-    each(1, col_count, greet(col_peer))
+    each(1, groups, greet(group_peer))
+    each(1, 2, greet(core_peer))
 
     owner = owner_ref[...]
     table = jnp.concatenate(
@@ -98,7 +103,7 @@
     for sub in range(sub_count):
         alive_col = (iota((prim, prim), 0) < counts_ref[sub]).astype(F32)
         alive_row = (iota((prim, prim), 1) < counts_ref[sub]).astype(F32)
-        schur = jnp.zeros((prim, prim), F32)
+        schur = jnp.zeros((prim, 2 * prim), F32)
         for k in range(face_sub):
             face = sub * face_sub + k
             if face % chunk == 0:
@@ -108,8 +113,8 @@
             basis_b = basis_buf[sub * elem_sub + faces_ref[1, face]].astype(F32)
             flux = dot(flux_buf[face], (basis_a + basis_b).astype(BF16))
             image = 0.5 * flux + (0.5 * diss_ref[face]) * (basis_a - basis_b)
-            schur = schur + dot(basis_first, image.astype(BF16), 0, 0)
-        schur = schur * alive_col * alive_row
+            schur = schur + dot(basis_first, jnp.concatenate(split2(image), axis=1), 0, 0)
+        schur = (schur[:, :prim] + schur[:, prim:]) * alive_col * alive_row
         flat = basis_buf[sub * elem_sub:(sub + 1) * elem_sub].reshape(elem_sub * units, prim)
         load_rows.append(dot(res_ref[sub:sub + 1, :], flat) * alive_row[:1])
         diag_rows.append(
@@ -122,7 +127,7 @@
     info_own[...] = jnp.concatenate(
         [jnp.concatenate(part, axis=1) for part in (load_rows, diag_rows, highs_f, lows_f)], axis=0
     )
-    pl.semaphore_wait(barrier, wide_count + col_count - 2)
+    pl.semaphore_wait(barrier, groups)
 
     def send(source, target, peer, index, count, hop):
         def act(k):
@@ -148,35 +153,32 @@
             return total + dot(jnp.concatenate(pieces, axis=0), lows[w], 1, 1)
 
         total = jnp.zeros((2 * parts * n, 128), F32)
-        if wide_count <= UNROLL:
-            for w in range(wide_count):
+        if groups <= UNROLL:
+            for w in range(groups):
                 total = add(w, total)
         else:
-            total = lax.fori_loop(0, wide_count, add, total)
+            total = lax.fori_loop(0, groups, add, total)
         return jnp.concatenate(
             [total[2 * i * n:(2 * i + 1) * n] + total[(2 * i + 1) * n:(2 * i + 2) * n] for i in range(parts)],
             axis=0,
         )
 
-    def col_sum(value, target, hop):
-        target[my_col] = value
-        send(target.at[my_col], target, col_peer, my_col, col_count, hop)
-        wait(target, col_count, recv_sem.at[hop])
-        total = target[0]
-        for c in range(1, col_count):
-            total = total + target[c]
-        return total
-
-    info[my_wide] = info_own[...]
-    send(info_own, info, wide_peer, my_wide, wide_count, 0)
-    wait(info, wide_count, recv_sem.at[0])
+    def core_sum(value, target, hop):
+        target[core] = value
+        send(target.at[core], target, core_peer, core, 2, hop)
+        wait(target, 2, recv_sem.at[hop])
+        return target[0] + target[1]
+
+    info[my_group] = info_own[...]
+    send(info_own, info, group_peer, my_group, groups, 0)
+    wait(info, groups, recv_sem.at[0])
 
     def prepare(w):
         hots[w] = hot(info[w, 2:3, :].astype(jnp.int32), n).astype(BF16)
         lows[w] = hot(info[w, 3:4, :].astype(jnp.int32), 128).astype(BF16)
 
-    each(0, wide_count, prepare)
-    total = col_sum(
+    each(0, groups, prepare)
+    total = core_sum(
         to_dense(lambda w: [info[w, 0:1, :], info[w, 1:2, :]], 2), dense0, 1
     )
     load = total[:n]
@@ -197,10 +199,10 @@
             values = jnp.concatenate([high[:, part], low[:, part], high[:, part]], axis=1)
             prods.append(dot(values, schurs[sub], 1, 1))
         row_own[rnd] = jnp.concatenate(prods, axis=1)
-        rows[rnd, my_wide] = row_own[rnd]
-        send(row_own.at[rnd], rows.at[rnd], wide_peer, my_wide, wide_count, 2 * rnd + 2)
-        wait(rows.at[rnd], wide_count, recv_sem.at[2 * rnd + 2])
-        total = col_sum(to_dense(lambda w: [rows[rnd, w]], 1), denses.at[rnd], 2 * rnd + 3)
+        rows[rnd, my_group] = row_own[rnd]
+        send(row_own.at[rnd], rows.at[rnd], group_peer, my_group, groups, 2 * rnd + 2)
+        wait(rows.at[rnd], groups, recv_sem.at[2 * rnd + 2])
+        total = core_sum(to_dense(lambda w: [rows[rnd, w]], 1), denses.at[rnd], 2 * rnd + 3)
         current = current + (load - total) * scale
 
     sol_ref[...] = rows_sum(
@@ -212,11 +214,11 @@
         flat = basis_buf[sub * elem_sub:(sub + 1) * elem_sub].reshape(elem_sub * units, prim)
         corr_ref[sub:sub + 1, :] = dot(near_sub, flat, 1, 1)
 
-    wait(info, wide_count, send_sem.at[0])
-    wait(dense0, col_count, send_sem.at[1])
+    wait(info, groups, send_sem.at[0])
+    wait(dense0, 2, send_sem.at[1])
     for rnd in range(ITERS):
-        wait(rows.at[rnd], wide_count, send_sem.at[2 * rnd + 2])
-        wait(denses.at[rnd], col_count, send_sem.at[2 * rnd + 3])
+        wait(rows.at[rnd], groups, send_sem.at[2 * rnd + 2])
+        wait(denses.at[rnd], 2, send_sem.at[2 * rnd + 3])
 
 
 def body(flux_jac, dissipation, basis, residual, face_elems, primal, coarse_owner, counts):
@@ -233,6 +235,7 @@
     vmem = pl.BlockSpec(memory_space=pltpu.VMEM)
     hbm = pl.BlockSpec(memory_space=pltpu.HBM)
     hops = 2 * ITERS + 2
+    groups = n // 2
     correction, own = pl.pallas_call(
         functools.partial(
             kernel,
@@ -248,20 +251,20 @@
             pltpu.VMEM(flux_jac.shape, BF16),
             pltpu.VMEM(basis.shape, BF16),
             pltpu.VMEM((4, row_count), F32),
-            pltpu.VMEM((wide_count, 4, row_count), F32),
+            pltpu.VMEM((groups, 4, row_count), F32),
             pltpu.VMEM((ITERS, 1, row_count), F32),
-            pltpu.VMEM((ITERS, wide_count, 1, row_count), F32),
-            pltpu.VMEM((wide_count, n, row_count), BF16),
-            pltpu.VMEM((wide_count, 128, row_count), BF16),
-            pltpu.VMEM((col_count, 2 * n, 128), F32),
-            pltpu.VMEM((ITERS, col_count, n, 128), F32),
+            pltpu.VMEM((ITERS, groups, 1, row_count), F32),
+            pltpu.VMEM((groups, n, row_count), BF16),
+            pltpu.VMEM((groups, 128, row_count), BF16),
+            pltpu.VMEM((2, 2 * n, 128), F32),
+            pltpu.VMEM((ITERS, 2, n, 128), F32),
             pltpu.SemaphoreType.DMA((hops,)),
             pltpu.SemaphoreType.DMA((hops,)),
             pltpu.SemaphoreType.DMA((face_count // chunk,)),
             pltpu.SemaphoreType.DMA,
         ],
         compiler_params=pltpu.CompilerParams(
-            collective_id=0, has_side_effects=True, vmem_limit_bytes=48 << 20
+            collective_id=0, has_side_effects=True, vmem_limit_bytes=60 << 20
         ),
         name="coarse",
     )(face_elems.T, dissipation, counts, residual, primal, coarse_owner.reshape(-1, 128), flux_jac, basis)

time: 49 us -> 40.4 us (0.82)
  Pallas kernels: 41.5 us -> 37 us
  local copies, waits for them, and re-layouts: 6.51 us -> 2.51 us
    pallas_call x1, Pallas kernels: 41.5 us -> 37 us  [body(): pl.pallas_call(functools.partial(kernel, (col_count, wide_count, sub_coun...]
    unnamed x16 -> x2, local copies, waits for them, and re-layouts: 6.51 us -> 2.51 us
where the time goes in v3:
time: 40.4 us; the launch traced here: 40.1 us
  Pallas kernels  37 us (92%)
  local copies, waits for them, and re-layouts  2.51 us (6%)
  between operations  0.64 us (2%)
    pallas_call x1, Pallas kernels, body(): pl.pallas_call(functools.partial(kernel, (col_count, wide_count, sub_coun...  37 us
    unnamed x2, local copies, waits for them, and re-layouts  2.51 us

profile of v3, /device:TPU:0, one launch (start us, length us, event | category | flops | bytes accessed | tf_op | source)
XLA Modules:
  0.0 40.1 jit_solution(9726853160058374848)
XLA Ops:
  0.6 37.0 %coarse.1 = (f32[2,2560]{1,0:T(2,128)}, f32[1,128]{1,0:T(1,128)}) custom-call(s32[2,24]{1,0:T(2,128)} %bitcast.4, f32[24]{0:T(128)} %diss_ref.1, s32[2]{0:T(128)} %counts_ref.1, bf16[2,2560]{1,0:T(2,128)(2,1)} %res_ref.1, s32[2,128]{1,0:T(2,128)} %primal_ref.1, s32[32,128]{1,0:T(8,128)} %bitcast.3, bf16[24,320,320]{2,1,0:T(8,128)(2,1)} %flux_ref.1, ...), custom_call_target="tpu_custom_call" | custom-call | tf_op jit(solution)/shard_map/coarse/pallas_call | solution.py:239
  37.6 1.3 %copy.12 = f32[2,2560]{1,0:T(2,128)} copy(f32[2,2560]{1,0:T(2,128)} %get-tuple-element.8) | data formatting | bytes 40960
  38.9 1.2 %copy.13 = f32[128]{0:T(128)} copy(f32[128]{0:T(128)} %bitcast.5) | data formatting | bytes 1024

commit v4 on v3

--- a/solution.py
+++ b/solution.py
@@ -230,7 +230,7 @@
     elem_sub = basis.shape[0] // sub_count
     units, prim = basis.shape[1:]
     row_count = sub_count * prim
-    chunk = 4
+    chunk = face_count // sub_count
     smem = pl.BlockSpec(memory_space=pltpu.SMEM)
     vmem = pl.BlockSpec(memory_space=pltpu.VMEM)
     hbm = pl.BlockSpec(memory_space=pltpu.HBM)

time: 40.4 us -> 38.8 us (0.960)
  Pallas kernels: 37 us -> 35.4 us
    pallas_call x1, Pallas kernels: 37 us -> 35.4 us  [body(): pl.pallas_call(functools.partial(kernel, (col_count, wide_count, sub_coun...]
where the time goes in v4:
time: 38.8 us; the launch traced here: 38.5 us
  Pallas kernels  35.4 us (91%)
  local copies, waits for them, and re-layouts  2.51 us (6%)
  between operations  0.64 us (2%)
    pallas_call x1, Pallas kernels, body(): pl.pallas_call(functools.partial(kernel, (col_count, wide_count, sub_coun...  35.4 us
    unnamed x2, local copies, waits for them, and re-layouts  2.51 us

profile of v4, /device:TPU:0, one launch (start us, length us, event | category | flops | bytes accessed | tf_op | source)
XLA Modules:
  0.0 38.5 jit_solution(473101348649649301)
XLA Ops:
  0.6 35.4 %coarse.1 = (f32[2,2560]{1,0:T(2,128)}, f32[1,128]{1,0:T(1,128)}) custom-call(s32[2,24]{1,0:T(2,128)} %bitcast.4, f32[24]{0:T(128)} %diss_ref.1, s32[2]{0:T(128)} %counts_ref.1, bf16[2,2560]{1,0:T(2,128)(2,1)} %res_ref.1, s32[2,128]{1,0:T(2,128)} %primal_ref.1, s32[32,128]{1,0:T(8,128)} %bitcast.3, bf16[24,320,320]{2,1,0:T(8,128)(2,1)} %flux_ref.1, ...), custom_call_target="tpu_custom_call" | custom-call | tf_op jit(solution)/shard_map/coarse/pallas_call | solution.py:239
  36.0 1.3 %copy.12 = f32[2,2560]{1,0:T(2,128)} copy(f32[2,2560]{1,0:T(2,128)} %get-tuple-element.8) | data formatting | bytes 40960
  37.3 1.2 %copy.13 = f32[128]{0:T(128)} copy(f32[128]{0:T(128)} %bitcast.5) | data formatting | bytes 1024
